TPU v7x, 32 devices: a whole 2x2x4 slice. The times are simulated.
32 devices in a mesh: dp: 4 (over y, x), fsdp: 8 (over z, core).
Axes of the slice: x: 2, y: 2, z: 4, core: 2. Of those that a mesh axis runs over, the one named last changes fastest.
Arguments:
- hidden: bfloat16 [16384, 1536], P(('dp', 'fsdp')), may hold values from -6 to 6
- lengths: int32 [512], P(('dp', 'fsdp')), may hold values from 1 to 32
- norm_gain: float32 [1536], replicated, may hold values from 0.1 to 1.9
- up_weight: bfloat16 [1536, 3072], P('fsdp'), may hold values from -0.15625 to 0.15625
- down_weight: bfloat16 [3072, 1536], P('fsdp'), may hold values from -0.109375 to 0.109375
- pool_gain: float32 [1536], replicated, may hold values from 0.1 to 1.9
- proj_weight: bfloat16 [1536, 768], P('fsdp'), may hold values from -1 to 1
- owners: int32 [512, 1], P(('dp', 'fsdp')), may hold values from 0 to 3; in each aligned block of 16 rows (0 to 15, 16 to 31, ...) at most 8 rows name the same one
Outputs:
- owned: bfloat16 [1024, 768], P(('dp', 'fsdp'))
Inputs may be any that keep to these rules, and one draw needn't show every extreme that they name: `owners`: in each aligned block of 16 passages no owner is named by more than 8 passages, a bound that some block reaches.
All inputs are finite; a program needn't handle non-finite values.
Results may differ from a plain program's by a relative error of at most 0.014.
Values may be sent and summed in bfloat16 or wider, within the bound.
A program may use at most 128 MiB of HBM per device.

v0:
```python
import jax
import jax.numpy as jnp
from jax import lax
from jax.sharding import PartitionSpec as P

ITERS = 4
RIDGE_TERM = 1.0
EPSILON = 1e-06
PRECISE = lax.Precision.HIGHEST


def rms_scale(values, gain_vector):
    return (
        values
        * lax.rsqrt(jnp.mean(values * values, axis=-1, keepdims=True) + EPSILON)
        * gain_vector
    )


def build_covariance(full_sums, average_sum, row_count):
    average = average_sum / row_count
    eye_matrix = jnp.eye(full_sums.shape[0], dtype=jnp.float32)
    covariance = (
        full_sums / row_count - average[:, None] * average[None, :] + RIDGE_TERM * eye_matrix
    )
    magnitude = jnp.sqrt(jnp.sum(covariance * covariance))
    initial = 4.0 / magnitude * eye_matrix - 4.0 * covariance / (magnitude * magnitude)
    return (covariance, average, initial)


def newton_update(iterate_rows, covariance, iterate_full):
    mixed = jnp.dot(
        jnp.dot(iterate_rows, covariance, precision=PRECISE, preferred_element_type=jnp.float32),
        iterate_full,
        precision=PRECISE,
        preferred_element_type=jnp.float32,
    )
    return 2.0 * iterate_rows - mixed


def last_update_rows(centered, covariance, iterate_full):
    row_product = jnp.dot(
        centered, iterate_full, precision=PRECISE, preferred_element_type=jnp.float32
    )
    row_mixed = jnp.dot(
        jnp.dot(row_product, covariance, precision=PRECISE, preferred_element_type=jnp.float32),
        iterate_full,
        precision=PRECISE,
        preferred_element_type=jnp.float32,
    )
    return 2.0 * row_product - row_mixed


def on_device(hidden, lengths, norm_gain, up_weight, down_weight, pool_gain, proj_weight, owners):
    tok_rows = hidden.shape[0]
    pass_rows = lengths.shape[0]
    seq_len = tok_rows // pass_rows
    normed = rms_scale(hidden.astype(jnp.float32), norm_gain).astype(jnp.bfloat16)
    columns = normed
    hidden_pre = jnp.dot(
        columns,
        lax.all_gather(up_weight, "fsdp", axis=0, tiled=True),
        preferred_element_type=jnp.float32,
    )
    activated = jax.nn.gelu(hidden_pre, approximate=True).astype(jnp.bfloat16)
    columns = activated
    branch = jnp.dot(
        columns,
        lax.all_gather(down_weight, "fsdp", axis=0, tiled=True),
        preferred_element_type=jnp.float32,
    )
    layer_out = (hidden.astype(jnp.float32) + branch).astype(jnp.bfloat16)
    token_index = lax.broadcasted_iota(jnp.int32, (pass_rows, tok_rows), 1)
    passage_index = lax.broadcasted_iota(jnp.int32, (pass_rows, tok_rows), 0)
    inside = (token_index // seq_len == passage_index) & (token_index % seq_len < lengths[:, None])
    pooled = (
        jnp.dot(inside.astype(jnp.bfloat16), layer_out, preferred_element_type=jnp.float32)
        / lengths.astype(jnp.float32)[:, None]
    )
    pool_normed = rms_scale(pooled, pool_gain).astype(jnp.bfloat16)
    columns = pool_normed
    embedded = jnp.dot(
        columns,
        lax.all_gather(proj_weight, "fsdp", axis=0, tiled=True),
        preferred_element_type=jnp.float32,
    )
    products = jnp.dot(embedded.T, embedded, precision=PRECISE, preferred_element_type=jnp.float32)
    column_sum = jnp.sum(embedded, axis=0)
    total_rows = float(pass_rows * lax.axis_size("dp") * lax.axis_size("fsdp"))
    full_sums, average_sum = lax.psum((products, column_sum), ("dp", "fsdp"))
    covariance, average, iterate_full = build_covariance(full_sums, average_sum, total_rows)
    for iteration in range(ITERS - 2):
        iterate_full = newton_update(iterate_full, covariance, iterate_full)
    whitened = last_update_rows(embedded - average, covariance, iterate_full).astype(jnp.bfloat16)
    owner_count = lax.axis_size("dp")
    capacity = 2 * pass_rows // owner_count
    target_owner = owners[:, 0]
    position = lax.broadcasted_iota(jnp.int32, (pass_rows, pass_rows), 0)
    previous = lax.broadcasted_iota(jnp.int32, (pass_rows, pass_rows), 1)
    earlier = (target_owner[:, None] == target_owner[None, :]) & (previous < position)
    target = target_owner * capacity + jnp.sum(earlier.astype(jnp.int32), axis=1)
    slot_index = lax.broadcasted_iota(jnp.int32, (owner_count * capacity, pass_rows), 0)
    selector = (slot_index == target[None, :]).astype(jnp.bfloat16)
    outgoing = jnp.dot(selector, whitened, preferred_element_type=jnp.float32).astype(jnp.bfloat16)
    return lax.all_to_all(outgoing, "dp", split_axis=0, concat_axis=0, tiled=True)


def solution(mesh):
    placed = (
        P(("dp", "fsdp"), None),
        P(("dp", "fsdp")),
        P(),
        P("fsdp", None),
        P("fsdp", None),
        P(),
        P("fsdp", None),
        P(("dp", "fsdp"), None),
    )
    return jax.shard_map(
        on_device, mesh=mesh, in_specs=placed, out_specs=P(("dp", "fsdp"), None), check_vma=False
    )
```

profile of v0, /device:TPU:0, one launch (start us, length us, event | category | flops | bytes accessed | tf_op | source)
XLA Modules:
  0.0 415.3 jit_solution(10799612231338822403)
XLA Ops:
  6.5 0.0 copy-start.3
  6.5 0.0 copy-start.1
  6.5 0.0 copy-start.4
  6.5 0.0 all-gather.4.cloned.1.call-start
  6.5 0.7 all-gather.4.cloned.1.call-update
  7.3 0.0 all-gather.6.cloned.1.call-start
  7.3 0.7 all-gather.6.cloned.1.call-update
  8.0 0.0 all-gather.8.cloned.1.call-start
  8.1 0.7 all-gather.8.cloned.1.call-update
  8.7 0.0 all-reduce.2.cloned.1.call-start
  8.8 0.0 copy-done.3
  8.8 0.0 copy-done.1
  8.9 0.4 fusion.8
  9.3 0.0 copy-start.2
  9.3 93.2 %all-gather.4.cloned.1.call-done = bf16[1536,3072]{1,0:T(8,128)(2,1)} async-done(((bf16[192,3072]{1,0:T(8,128)(2,1)}), bf16[1536,3072]{1,0:T(8,128)(2,1)}) %all-gather.4.cloned.1.call-update) | async-done | bytes 9437200 | tf_op jit(solution)/shard_map/all_gather | solution.py:62
  102.5 90.9 %all-gather.6.cloned.1.call-done = bf16[3072,1536]{1,0:T(8,128)(2,1)} async-done(((bf16[384,1536]{1,0:T(8,128)(2,1)}), bf16[3072,1536]{1,0:T(8,128)(2,1)}) %all-gather.6.cloned.1.call-update) | async-done | bytes 9437200 | tf_op jit(solution)/shard_map/all_gather | solution.py:69
  193.3 0.0 copy-done.4
  193.3 16.5 %fusion.16 = bf16[512,1536]{1,0:T(8,128)(2,1)S(1)} fusion(bf16[3072,1536]{1,0:T(8,128)(2,1)} %all-gather.6.cloned.1.call-done, bf16[512,1536]{1,0:T(8,128)(2,1)S(1)} %copy-done.1, bf16[1536,3072]{1,0:T(8,128)(2,1)} %all-gather.4.cloned.1.call-done, f32[1536]{0:T(1024)S(1)} %copy-done.4, f32[512]{0:T(512)S(1)} %add_rsqrt_fusion), kind=kOutput, calls=%fused_computation.19 | convolution fusion | flops 9683337216 | bytes 22028288 | tf_op jit(solution)/shard_map/dot_general | solution.py:67
  209.8 0.5 multiply_reduce_fusion.1
  210.3 14.8 %all-gather.8.cloned.1.call-done = bf16[1536,768]{1,0:T(8,128)(2,1)} async-done(((bf16[192,768]{1,0:T(8,128)(2,1)}), bf16[1536,768]{1,0:T(8,128)(2,1)}) %all-gather.8.cloned.1.call-update) | async-done | bytes 2359312 | tf_op jit(solution)/shard_map/all_gather | solution.py:84
  225.1 0.0 copy-done.2
  225.1 2.1 fusion.73
  227.2 0.0 copy-start.5
  227.2 3.5 fusion.74
  230.7 0.0 all-reduce.2.cloned.1.call-update
  230.7 0.0 copy-done.5
  230.7 0.2 convert_reduce_fusion
  230.9 40.2 %psum.14 = f32[768]{0:T(1024)S(1)} all-reduce(f32[768]{0:T(1024)S(1)} %get-tuple-element.7), channel_id=1, replica_groups=mesh['dp'=4,'fsdp'=8] {'dp','fsdp'}, use_global_device_ids=true, to_apply=%region_4.5 | all-reduce | flops 768 | bytes 6144 | tf_op jit(solution)/shard_map/psum | solution.py:90
  271.2 94.1 %all-reduce.2.cloned.1.call-done = f32[768,768]{1,0:T(8,128)} async-done(((f32[768,768]{1,0:T(8,128)}), f32[768,768]{1,0:T(8,128)}) %all-reduce.2.cloned.1.call-update) | async-done | bytes 2359312 | tf_op jit(solution)/shard_map/psum | solution.py:90
  365.3 0.0 copy-start
  365.3 3.2 multiply_reduce_fusion
  369.2 0.0 copy-done
  369.3 6.7 %fusion.19 = f32[768,768]{1,0:T(8,128)S(1)} fusion(f32[]{:T(128)S(6)} %mul.135, f32[]{:T(128)S(6)} %div.58, f32[768,768]{1,0:T(8,128)S(1)} %copy-done, f32[768]{0:T(1024)S(1)} %broadcast_multiply_fusion), kind=kOutput, calls=%fused_computation.27 | convolution fusion | flops 5445255168 | bytes 4721672 | tf_op jit(solution)/shard_map/dot_general | solution.py:33
  376.0 6.9 %multiply_subtract_fusion.1 = f32[768,768]{1,0:T(8,128)S(1)} fusion(f32[768,768]{1,0:T(8,128)S(1)} %fusion.19, f32[]{:T(128)S(6)} %mul.135, f32[]{:T(128)S(6)} %div.58, f32[768]{0:T(1024)S(1)} %broadcast_multiply_fusion, f32[768,768]{1,0:T(8,128)S(1)} %copy-done), kind=kOutput, calls=%fused_computation.21 | convolution fusion | flops 5448794112 | bytes 7080968 | tf_op jit(solution)/shard_map/dot_general | solution.py:32
  382.9 6.4 %fusion.72 = f32[768,768]{1,0:T(8,128)S(1)} fusion(f32[768,768]{1,0:T(8,128)S(1)} %multiply_subtract_fusion.1, f32[768,768]{1,0:T(8,128)S(1)} %copy-done, f32[768]{0:T(1024)S(1)} %broadcast_multiply_fusion), kind=kOutput, calls=%fused_computation.89 | convolution fusion | flops 5439356928 | bytes 7080960 | tf_op jit(solution)/shard_map/dot_general | solution.py:33
  389.3 6.1 %multiply_subtract_fusion = f32[768,768]{1,0:T(8,128)S(1)} fusion(f32[768,768]{1,0:T(8,128)S(1)} %multiply_subtract_fusion.1, f32[768,768]{1,0:T(8,128)S(1)} %fusion.72), kind=kOutput, calls=%fused_computation.20 | convolution fusion | flops 5436997632 | bytes 7077888 | tf_op jit(solution)/shard_map/dot_general | solution.py:32
  395.4 1.5 fusion.41
  396.8 1.6 fusion.71
  398.4 1.3 fusion.39
  399.7 0.1 fusion.38
  399.8 8.1 %all_to_all.12 = bf16[4,8,768]{2,1,0:T(8,128)(2,1)S(1)} all-to-all(bf16[4,8,768]{2,1,0:T(8,128)(2,1)S(1)} %fusion.38), channel_id=1, replica_groups=mesh['dp'=4,'fsdp'=8] {'dp'}, dimensions={0} | all-to-all | bytes 98304 | tf_op jit(solution)/shard_map/all_to_all | solution.py:105
  407.9 0.6 copy.11
  (8 shorter events, 0.0 us)
Async XLA Ops:
  6.5 2.3 copy-start.3
  6.5 2.3 copy-start.1
  6.5 186.8 %copy-start.4 = (f32[1536]{0:T(1024)S(1)}, f32[1536]{0:T(1024)}, u32[]{:S(2)}) copy-start(f32[1536]{0:T(1024)} %param.10) | copy-start | bytes 18436
  6.5 95.9 %all-gather.4.cloned.1.call-start = ((), (), s32[]{:S(2)}) async-start(), calls=%async_computation.1 | async-start | bytes 10616832 | tf_op jit(solution)/shard_map/all_gather | solution.py:62
  7.3 186.1 %all-gather.6.cloned.1.call-start = ((), (), s32[]{:S(2)}) async-start(), calls=%async_computation.2 | async-start | bytes 10616832 | tf_op jit(solution)/shard_map/all_gather | solution.py:69
  8.0 217.1 %all-gather.8.cloned.1.call-start = ((), (), s32[]{:S(2)}) async-start(), calls=%async_computation.3 | async-start | bytes 2654208 | tf_op jit(solution)/shard_map/all_gather | solution.py:84
  8.7 356.5 %all-reduce.2.cloned.1.call-start = ((), (), s32[]{:S(2)}) async-start(), calls=%async_computation.4 | async-start | bytes 4718592 | tf_op jit(solution)/shard_map/psum | solution.py:90
  9.3 215.8 %copy-start.2 = (f32[1536]{0:T(1024)S(1)}, f32[1536]{0:T(1024)}, u32[]{:S(2)}) copy-start(f32[1536]{0:T(1024)} %param.13) | copy-start | bytes 18436
  227.2 3.5 copy-start.5
  365.3 4.0 copy-start
Sparse Core Ops, SparseCore 0:
  9.0 93.4 all-gather.3
  104.1 89.1 all-gather.5
  195.0 30.0 all-gather.7
  230.8 134.3 all-reduce.1
where the time goes:
time: 424 us; the launch traced here: 415 us
  waiting for transfers between devices  295 us (70%)
  matrix products  53.1 us (13%)
  blocking collectives  48.4 us (11%)
  between operations  14.2 us (3%)
    psum x1, waiting for transfers between devices, on_device(): full_sums, average_sum = lax.psum((products, column_sum), ('dp', 'fsdp'))  94.1 us
    all_gather x1, waiting for transfers between devices, on_device(): lax.all_gather(up_weight, 'fsdp', axis=0, tiled=True)  93.2 us
    all_gather x1, waiting for transfers between devices, on_device(): lax.all_gather(down_weight, 'fsdp', axis=0, tiled=True)  90.9 us
    psum x1, blocking collectives, on_device(): full_sums, average_sum = lax.psum((products, column_sum), ('dp', 'fsdp'))  40.2 us
    dot_general x1, matrix products, on_device(): jnp.dot(columns, lax.all_gather(down_weight, 'fsdp', axis=0, tiled=True),...  16.5 us
    all_gather x1, waiting for transfers between devices, on_device(): lax.all_gather(proj_weight, 'fsdp', axis=0, tiled=True)  14.8 us
    dot_general x2, matrix products, newton_update(): jnp.dot(iterate_rows, covariance, precision=PRECISE, preferred_element_ty...  13.1 us
    dot_general x2, matrix products, newton_update(): jnp.dot(jnp.dot(iterate_rows, covariance, precision=PRECISE, preferred_el...  13 us
  transfers between devices with their start and end apart: 4, of which 4 were waited for; matrix products, arithmetic and copies ran while one was open for 4% of the time, Pallas kernels for 0%

commit v1 on v0

--- a/solution.py
+++ b/solution.py
@@ -7,6 +7,27 @@
 RIDGE_TERM = 1.0
 EPSILON = 1e-06
 PRECISE = lax.Precision.HIGHEST
+
+
+def laid_out(blocks, dim):
+    lengths = list(blocks.shape[1:])
+    lengths[dim] *= blocks.shape[0]
+    return jnp.moveaxis(blocks, 0, dim).reshape(lengths)
+
+
+def grow_blocks(x, axis):
+    size, place = (lax.axis_size(axis), lax.axis_index(axis))
+    blocks, bit = (x[None], 1)
+    while bit < size:
+        other = lax.ppermute(blocks, axis, [(i, i ^ bit) for i in range(size)])
+        low = place & bit == 0
+        blocks = jnp.concatenate([jnp.where(low, blocks, other), jnp.where(low, other, blocks)])
+        bit *= 2
+    return blocks
+
+
+def doubled_up(x, axis, dim):
+    return laid_out(grow_blocks(x, axis), dim)
 
 
 def rms_scale(values, gain_vector):
@@ -58,9 +79,7 @@
     normed = rms_scale(hidden.astype(jnp.float32), norm_gain).astype(jnp.bfloat16)
     columns = normed
     hidden_pre = jnp.dot(
-        columns,
-        lax.all_gather(up_weight, "fsdp", axis=0, tiled=True),
-        preferred_element_type=jnp.float32,
+        columns, doubled_up(up_weight, "fsdp", 0), preferred_element_type=jnp.float32
     )
     activated = jax.nn.gelu(hidden_pre, approximate=True).astype(jnp.bfloat16)
     columns = activated

time: 424 us -> 599 us (1.41)
  waiting for transfers between devices: 295 us -> 448 us
  other arithmetic: 3.85 us -> 19.4 us
    ppermute x0 -> x3, waiting for transfers between devices: none -> 351 us  [grow_blocks(): other = lax.ppermute(blocks, axis, [(i, i ^ bit) for i in range(size)])]
    all_gather x1 -> x0, waiting for transfers between devices: 93.2 us -> none  [on_device(): lax.all_gather(up_weight, 'fsdp', axis=0, tiled=True)]
    all_gather x1, waiting for transfers between devices: 90.9 us -> 0.01 us  [on_device(): lax.all_gather(down_weight, 'fsdp', axis=0, tiled=True)]
    all_gather x1, waiting for transfers between devices: 14.8 us -> 0.02 us  [on_device(): lax.all_gather(proj_weight, 'fsdp', axis=0, tiled=True)]
    select_n x0 -> x3, other arithmetic: none -> 7.07 us  [grow_blocks(): jnp.where(low, blocks, other)]
    concatenate x0 -> x3, other arithmetic: none -> 7.04 us  [grow_blocks(): jnp.concatenate([jnp.where(low, blocks, other), jnp.where(low, other, blo...]
  transfers between devices with their start and end apart: 4 -> 6, of which waited for: 4 -> 4; matrix products, arithmetic and copies ran while one was open for 4% -> 6% of each run, Pallas kernels for 0% -> 0%
where the time goes in v1:
time: 599 us; the launch traced here: 589 us
  waiting for transfers between devices  448 us (75%)
  matrix products  53 us (9%)
  blocking collectives  47.3 us (8%)
  other arithmetic  19.4 us (3%)
  between operations  14.5 us (2%)
    ppermute x3, waiting for transfers between devices, grow_blocks(): other = lax.ppermute(blocks, axis, [(i, i ^ bit) for i in range(size)])  351 us
    psum x1, waiting for transfers between devices, on_device(): full_sums, average_sum = lax.psum((products, column_sum), ('dp', 'fsdp'))  96.3 us
    psum x1, blocking collectives, on_device(): full_sums, average_sum = lax.psum((products, column_sum), ('dp', 'fsdp'))  39.1 us
    dot_general x1, matrix products, on_device(): jnp.dot(columns, lax.all_gather(down_weight, 'fsdp', axis=0, tiled=True),...  16.5 us
    dot_general x2, matrix products, newton_update(): jnp.dot(iterate_rows, covariance, precision=PRECISE, preferred_element_ty...  13.1 us
    dot_general x2, matrix products, newton_update(): jnp.dot(jnp.dot(iterate_rows, covariance, precision=PRECISE, preferred_el...  12.9 us
  transfers between devices with their start and end apart: 6, of which 4 were waited for; matrix products, arithmetic and copies ran while one was open for 6% of the time, Pallas kernels for 0%

profile of v1, /device:TPU:0, one launch (start us, length us, event | category | flops | bytes accessed | tf_op | source)
XLA Modules:
  0.0 589.1 jit_solution(15190138149387936655)
XLA Ops:
  6.5 0.0 all-gather.3.cloned.1.call-start
  6.5 0.7 all-gather.3.cloned.1.call-update
  7.3 0.0 all-gather.5.cloned.1.call-start
  7.3 0.5 collective-permute-start
  7.8 2.7 collective-permute-done
  10.5 1.4 broadcast_select_fusion.5
  11.9 0.0 copy-start.1
  11.9 0.2 pad_maximum_fusion.2
  12.2 0.8 copy-done.1
  13.0 2.9 collective-permute-start.1
  15.9 127.5 %collective-permute-done.1 = bf16[2,192,3072]{2,1,0:T(8,128)(2,1)} collective-permute-done((bf16[2,192,3072]{2,1,0:T(8,128)(2,1)S(1)}, bf16[2,192,3072]{2,1,0:T(8,128)(2,1)}, u32[]{:S(2)}, u32[]{:S(2)}) %collective-permute-start.1) | collective-permute-done | bytes 2359328 | tf_op jit(solution)/shard_map/ppermute | solution.py:22
  143.4 2.3 broadcast_select_fusion.3
  145.7 0.0 copy-start
  145.7 0.0 copy-start.5
  145.7 2.8 pad_maximum_fusion.1
  148.5 0.0 copy-done
  148.6 1.7 collective-permute-start.2
  150.3 0.0 all-gather.5.cloned.1.call-update
  150.3 0.0 all-reduce.2.cloned.1.call-start
  150.4 0.0 copy-done.5
  150.4 1.8 fusion.8
  152.2 220.9 %collective-permute-done.2 = bf16[4,192,3072]{2,1,0:T(8,128)(2,1)} collective-permute-done((bf16[4,192,3072]{2,1,0:T(8,128)(2,1)}, bf16[4,192,3072]{2,1,0:T(8,128)(2,1)}, u32[]{:S(2)}, u32[]{:S(2)}) %collective-permute-start.2) | collective-permute-done | bytes 4718624 | tf_op jit(solution)/shard_map/ppermute | solution.py:22
  373.2 3.4 broadcast_select_fusion.1
  376.5 0.0 copy-start.3
  376.6 0.0 copy-start.6
  376.6 4.0 pad_maximum_fusion
  380.6 0.0 all-gather.3.cloned.1.call-done
  380.6 0.0 copy-done.3
  380.6 0.0 copy-done.6
  380.6 0.0 copy-start.4
  380.6 16.5 %fusion.16 = bf16[512,1536]{1,0:T(8,128)(2,1)S(1)} fusion(bf16[3072,1536]{1,0:T(8,128)(2,1)} %all-gather.3.cloned.1.call-done, bf16[512,1536]{1,0:T(8,128)(2,1)S(1)} %copy-done.3, bf16[1536,3072]{1,0:T(8,128)(2,1)} %bitcast.24, f32[1536]{0:T(1024)S(1)} %copy-done.6, f32[512]{0:T(512)S(1)} %add_rsqrt_fusion), kind=kOutput, calls=%fused_computation.23 | convolution fusion | flops 9683337216 | bytes 22028288 | tf_op jit(solution)/shard_map/dot_general | solution.py:86
  397.1 0.5 multiply_reduce_fusion.1
  397.6 0.0 all-gather.5.cloned.1.call-done
  397.6 0.0 copy-done.4
  397.6 2.1 fusion.73
  399.8 0.0 copy-start.7
  399.8 3.5 fusion.74
  403.2 0.0 all-reduce.2.cloned.1.call-update
  403.3 0.0 copy-done.7
  403.3 0.2 convert_reduce_fusion
  403.5 39.1 %psum.14 = f32[768]{0:T(1024)S(1)} all-reduce(f32[768]{0:T(1024)S(1)} %get-tuple-element.13), channel_id=1, replica_groups=mesh['dp'=4,'fsdp'=8] {'dp','fsdp'}, use_global_device_ids=true, to_apply=%region_4.5 | all-reduce | flops 768 | bytes 6144 | tf_op jit(solution)/shard_map/psum | solution.py:109
  442.6 96.3 %all-reduce.2.cloned.1.call-done = f32[768,768]{1,0:T(8,128)} async-done(((f32[768,768]{1,0:T(8,128)}), f32[768,768]{1,0:T(8,128)}) %all-reduce.2.cloned.1.call-update) | async-done | bytes 2359312 | tf_op jit(solution)/shard_map/psum | solution.py:109
  538.9 0.0 copy-start.2
  538.9 3.2 multiply_reduce_fusion
  542.8 0.0 copy-done.2
  542.9 6.7 %fusion.19 = f32[768,768]{1,0:T(8,128)S(1)} fusion(f32[]{:T(128)S(6)} %mul.135, f32[]{:T(128)S(6)} %div.58, f32[768,768]{1,0:T(8,128)S(1)} %copy-done.2, f32[768]{0:T(1024)S(1)} %broadcast_multiply_fusion), kind=kOutput, calls=%fused_computation.34 | convolution fusion | flops 5445255168 | bytes 4721672 | tf_op jit(solution)/shard_map/dot_general | solution.py:54
  549.6 6.9 %multiply_subtract_fusion.1 = f32[768,768]{1,0:T(8,128)S(1)} fusion(f32[768,768]{1,0:T(8,128)S(1)} %fusion.19, f32[]{:T(128)S(6)} %mul.135, f32[]{:T(128)S(6)} %div.58, f32[768]{0:T(1024)S(1)} %broadcast_multiply_fusion, f32[768,768]{1,0:T(8,128)S(1)} %copy-done.2), kind=kOutput, calls=%fused_computation.26 | convolution fusion | flops 5448794112 | bytes 7080968 | tf_op jit(solution)/shard_map/dot_general | solution.py:53
  556.5 6.4 %fusion.72 = f32[768,768]{1,0:T(8,128)S(1)} fusion(f32[768,768]{1,0:T(8,128)S(1)} %multiply_subtract_fusion.1, f32[768,768]{1,0:T(8,128)S(1)} %copy-done.2, f32[768]{0:T(1024)S(1)} %broadcast_multiply_fusion), kind=kOutput, calls=%fused_computation.98 | convolution fusion | flops 5439356928 | bytes 7080960 | tf_op jit(solution)/shard_map/dot_general | solution.py:54
  562.8 6.1 %multiply_subtract_fusion = f32[768,768]{1,0:T(8,128)S(1)} fusion(f32[768,768]{1,0:T(8,128)S(1)} %multiply_subtract_fusion.1, f32[768,768]{1,0:T(8,128)S(1)} %fusion.72), kind=kOutput, calls=%fused_computation.25 | convolution fusion | flops 5436997632 | bytes 7077888 | tf_op jit(solution)/shard_map/dot_general | solution.py:53
  568.9 1.5 fusion.41
  570.4 1.6 fusion.71
  572.0 1.3 fusion.39
  573.2 0.1 fusion.38
  573.4 8.1 %all_to_all.12 = bf16[4,8,768]{2,1,0:T(8,128)(2,1)S(1)} all-to-all(bf16[4,8,768]{2,1,0:T(8,128)(2,1)S(1)} %fusion.38), channel_id=1, replica_groups=mesh['dp'=4,'fsdp'=8] {'dp'}, dimensions={0} | all-to-all | bytes 98304 | tf_op jit(solution)/shard_map/all_to_all | solution.py:124
  581.5 0.6 copy.11
  (8 shorter events, 0.0 us)
Async XLA Ops:
  6.5 374.1 %all-gather.3.cloned.1.call-start = ((), (), s32[]{:S(2)}) async-start(), calls=%async_computation.1 | async-start | bytes 10616832 | tf_op jit(solution)/shard_map/all_gather | solution.py:88
  7.3 390.3 %all-gather.5.cloned.1.call-start = ((), (), s32[]{:S(2)}) async-start(), calls=%async_computation.2 | async-start | bytes 2654208 | tf_op jit(solution)/shard_map/all_gather | solution.py:103
  7.3 3.2 collective-permute-start
  11.9 1.0 copy-start.1
  13.0 130.4 %collective-permute-start.1 = (bf16[2,192,3072]{2,1,0:T(8,128)(2,1)S(1)}, bf16[2,192,3072]{2,1,0:T(8,128)(2,1)}, u32[]{:S(2)}, u32[]{:S(2)}) collective-permute-start(bf16[2,192,3072]{2,1,0:T(8,128)(2,1)S(1)} %pad_maximum_fusion.2), channel_id=1, source_target_pairs={{0,2},{1,3},{2,0},{3,1},{4,6},{5,7},{6,4},{7,5},{8,10},{9,11},{10,... | collective-permute-start | bytes 7077896 | tf_op jit(solution)/shard_map/ppermute | solution.py:22
  145.7 2.8 copy-start
  145.7 4.7 copy-start.5
  148.6 224.6 %collective-permute-start.2 = (bf16[4,192,3072]{2,1,0:T(8,128)(2,1)}, bf16[4,192,3072]{2,1,0:T(8,128)(2,1)}, u32[]{:S(2)}, u32[]{:S(2)}) collective-permute-start(bf16[4,192,3072]{2,1,0:T(8,128)(2,1)} %pad_maximum_fusion.1), channel_id=1, source_target_pairs={{0,4},{1,5},{2,6},{3,7},{4,0},{5,1},{6,2},{7,3},{8,12},{9,13},{10,... | collective-permute-start | bytes 14155784 | tf_op jit(solution)/shard_map/ppermute | solution.py:22
  150.3 388.5 %all-reduce.2.cloned.1.call-start = ((), (), s32[]{:S(2)}) async-start(), calls=%async_computation.3 | async-start | bytes 4718592 | tf_op jit(solution)/shard_map/psum | solution.py:109
  376.5 4.1 copy-start.3
  376.6 4.1 copy-start.6
  380.6 17.0 %copy-start.4 = (f32[1536]{0:T(1024)S(1)}, f32[1536]{0:T(1024)}, u32[]{:S(2)}) copy-start(f32[1536]{0:T(1024)} %param.13) | copy-start | bytes 18436
  399.8 3.5 copy-start.7
  538.9 4.0 copy-start.2
Sparse Core Ops, SparseCore 0:
  9.0 133.6 all-gather.2
  150.4 133.4 all-gather.4
  403.4 135.4 all-reduce.1
